TPU v7x, 256 devices: a whole 4x4x8 slice. The times are simulated.
256 devices in a mesh: seq: 128 (over y, x, z), head: 2 (over core).
Axes of the slice: x: 4, y: 4, z: 8, core: 2. Of those that a mesh axis runs over, the one named last changes fastest.
Arguments:
- tokens: bfloat16 [32768, 2048], P('seq'), may hold values from -6 to 6
- dest: int32 [32768], P('seq'), may hold values from 0 to 32767, as said below
- segment_ids: int32 [32768], P('seq'), may hold values from 0 to 255, never falling along the last dimension, each value on 1 to 1024 neighbouring positions
- gain: float32 [2048], replicated, may hold values from 0.1 to 1.9
- w_qkv: bfloat16 [2048, 3, 1024], P(None, None, 'head')
- w_out: bfloat16 [1024, 2048], P('head'), may hold values from -0.1875 to 0.1875
Outputs:
- layer_out: bfloat16 [32768, 2048], P('seq', 'head')
Inputs may be any that keep to these rules, and one draw needn't show every extreme that they name: dest is a permutation of the sequence positions; the rows of one shard send exactly 2 rows to each shard's block of 256 positions.
All inputs are finite; a program needn't handle non-finite values.
Results may differ from a plain program's by a relative error of at most 0.017.
The roundings to bfloat16 on the way count: a program that leaves them out, or rounds other values in their place, can miss the bound.
Values may be sent and summed in bfloat16 or wider, within the bound.
A program may use at most 128 MiB of HBM per device.

v0:
```python
import jax
import jax.numpy as jnp
from jax import lax
from jax.sharding import PartitionSpec as P

DH = 128
POOL = 16
LEVELS = 4


def extended(x, sides, width):
    for axis, dim in sides:
        count, length = (lax.axis_size(axis), x.shape[dim])
        up = [(i, (i + 1) % count) for i in range(count - 1)]
        down = [(j, i) for i, j in up]
        last = lax.slice_in_dim(x, length - width, length, axis=dim)
        initial = lax.slice_in_dim(x, 0, width, axis=dim)
        before = lax.ppermute(last, axis, up)
        after = lax.ppermute(initial, axis, down)
        x = jnp.concatenate([before, x, after], axis=dim)
    return x


def from_partner(block, axis, apart):
    count = lax.axis_size(axis)
    route = []
    for low in range(count):
        high = low | 1 << apart
        if high != low and high < count:
            route += [(low, high), (high, low)]
    return lax.ppermute(block, axis, route)


def rms_norm(rows_in, gain):
    values = rows_in.astype(jnp.float32)
    scaled = values * lax.rsqrt(jnp.mean(values * values, axis=-1, keepdims=True) + 1e-05) * gain
    return scaled.astype(jnp.bfloat16)


def project(normed, w_qkv):
    width = w_qkv.shape[0]
    return jnp.dot(normed, w_qkv.reshape(width, -1), preferred_element_type=jnp.float32).astype(
        jnp.bfloat16
    )


def pair_mean(stacked):
    pooled_count = stacked.shape[0] // 2
    return stacked.reshape(pooled_count, 2, stacked.shape[1], stacked.shape[2]).mean(1)


def shards(tokens, dest, segment_ids, gain, w_qkv, w_out):
    shard_count = lax.axis_size("seq")
    row_count = tokens.shape[0]
    peer_rows = row_count // shard_count
    my_index = lax.axis_index("seq")
    group_width = w_qkv.shape[2]
    local_heads = group_width // DH
    pooled_count = row_count // POOL
    normed = rms_norm(tokens, gain)
    shard_of = dest // row_count
    ordering = jnp.argsort(shard_of, stable=True)
    sent_pos = dest[ordering].reshape(shard_count, peer_rows)
    sending = normed[ordering].reshape(shard_count, peer_rows, -1)
    arrived, got_pos = (
        lax.all_to_all(sending, "seq", split_axis=0, concat_axis=0, tiled=True),
        lax.all_to_all(sent_pos, "seq", split_axis=0, concat_axis=0, tiled=True),
    )
    local_rows = got_pos.reshape(-1) - my_index * row_count
    placed = jnp.zeros_like(normed).at[local_rows].set(arrived.reshape(row_count, -1))
    qkv = project(placed, w_qkv)
    qkv = qkv.reshape(row_count, 3, group_width)
    queries = qkv[:, 0].reshape(row_count, local_heads, DH)
    keys_values = qkv[:, 1:]
    rims = extended(keys_values, (("seq", 0),), row_count)
    id_halo = extended(segment_ids + 1, (("seq", 0),), row_count)
    pooled = keys_values.astype(jnp.float32).reshape(pooled_count, POOL, 2, group_width).mean(1)
    siblings = []
    summary = pooled
    for level in range(LEVELS):
        partner = from_partner(summary, "seq", level)
        siblings.append(partner)
        upper_side = jnp.bitwise_and(jnp.right_shift(my_index, level), 1) == 1
        lower_half = jnp.where(upper_side, partner, summary)
        upper_half = jnp.where(upper_side, summary, partner)
        summary = pair_mean(jnp.concatenate([lower_half, upper_half], axis=0))
    coarse = jnp.concatenate(siblings, axis=0)
    coarse_keys = coarse[:, 0].reshape(-1, local_heads, DH)
    coarse_values = coarse[:, 1].reshape(-1, local_heads, DH)
    level_bias = jnp.concatenate(
        [
            jnp.full((pooled_count,), jnp.log(float(POOL * 2**level)), jnp.float32)
            for level in range(LEVELS)
        ]
    )
    score_scale = DH ** (-0.5)
    near_keys = rims[:, 0].reshape(3 * row_count, local_heads, DH)
    near_values = rims[:, 1].reshape(3 * row_count, local_heads, DH)
    fine = (
        jnp.einsum("thd,khd->htk", queries, near_keys, preferred_element_type=jnp.float32)
        * score_scale
    )
    same_doc = (segment_ids + 1)[:, None] == id_halo[None, :]
    fine = jnp.where(same_doc[None], fine, -jnp.inf)
    query_float = queries.astype(jnp.float32)
    coarse_scores = (
        jnp.einsum("thd,khd->htk", query_float, coarse_keys, precision=lax.Precision.HIGHEST)
        * score_scale
        + level_bias
    )
    top_score = jnp.maximum(jnp.max(fine, axis=-1), jnp.max(coarse_scores, axis=-1))
    fine_weights = jnp.exp(fine - top_score[..., None])
    coarse_weights = jnp.exp(coarse_scores - top_score[..., None])
    denominator = jnp.sum(fine_weights, axis=-1) + jnp.sum(coarse_weights, axis=-1)
    rounded = fine_weights.astype(jnp.bfloat16)
    numerator = jnp.einsum("htk,khd->thd", rounded, near_values, preferred_element_type=jnp.float32)
    numerator = numerator + jnp.einsum(
        "htk,khd->thd", coarse_weights, coarse_values, precision=lax.Precision.HIGHEST
    )
    attn = (
        (numerator / jnp.transpose(denominator)[..., None])
        .astype(jnp.bfloat16)
        .reshape(row_count, group_width)
    )
    partial_out = jnp.dot(attn, w_out, preferred_element_type=jnp.float32)
    return lax.psum_scatter(partial_out, "head", scatter_dimension=1, tiled=True).astype(
        jnp.bfloat16
    )


def solution(mesh):
    in_specs = (P("seq", None), P("seq"), P("seq"), P(), P(None, None, "head"), P("head", None))
    out_specs = P("seq", "head")
    return jax.shard_map(shards, mesh=mesh, in_specs=in_specs, out_specs=out_specs, check_vma=False)
```

profile of v0, /device:TPU:1, one launch (start us, length us, event | category | flops | bytes accessed | tf_op | source)
XLA Modules:
  0.0 173.3 jit_solution(9600769329420497482)
XLA Ops:
  6.5 0.8 and_select_fusion
  7.4 3.2 %sort.17 = (s32[256]{0:T(256)}, s32[256]{0:T(256)S(1)}) sort(s32[256]{0:T(256)S(1)} %and_select_fusion, s32[256]{0:T(256)S(1)} %iota.4), dimensions={0}, to_apply=%region_0.0 | sort | flops 2048 | bytes 4096 | tf_op jit(solution)/shard_map/jit(argsort)/sort | solution.py:62
  10.6 2.0 %gather_fusion = s32[256]{0:T(256)S(1)} fusion(s32[256]{0:T(256)} %param.7, s32[1024]{0:T(1024)S(1)} %pad_clamp_fusion), kind=kCustom, calls=%fused_computation | custom fusion | bytes 3072 | tf_op jit(solution)/shard_map/gather | solution.py:63
  12.5 0.8 all_to_all.9
  13.3 16.3 %all-to-all-start = ((s32[128,1,2]{2,1,0:T(1,128)}), s32[128,1,2]{2,1,0:T(1,128)S(1)}, u32[]{:S(2)}, u32[]{:S(2)}) async-start(s32[128,1,2]{2,1,0:T(1,128)} %bitcast), calls=%async_computation | async-start | bytes 131072 | tf_op jit(solution)/shard_map/all_to_all | solution.py:67
  29.7 1.5 fusion.3
  31.2 1.5 fusion.5
  32.7 2.3 %gather_fusion.1 = bf16[256,2048]{1,0:T(8,128)(2,1)} fusion(bf16[256,2048]{1,0:T(8,128)(2,1)S(1)} %fusion.5, s32[1024]{0:T(1024)S(1)} %pad_clamp_fusion), kind=kCustom, calls=%fused_computation.1 | custom fusion | bytes 2098176 | tf_op jit(solution)/shard_map/gather | solution.py:64
  35.1 2.6 %reshape.99 = bf16[128,2,2048]{2,1,0:T(2,128)(2,1)} reshape(bf16[256,2048]{1,0:T(8,128)(2,1)} %gather_fusion.1) | data formatting | bytes 2097152 | tf_op jit(solution)/shard_map/reshape | solution.py:64
  37.6 2.5 %all-to-all-done = s32[128,1,2]{2,1,0:T(1,128)S(1)} async-done(((s32[128,1,2]{2,1,0:T(1,128)}), s32[128,1,2]{2,1,0:T(1,128)S(1)}, u32[]{:S(2)}, u32[]{:S(2)}) %all-to-all-start) | async-done | bytes 1056 | tf_op jit(solution)/shard_map/all_to_all | solution.py:67
  40.1 10.7 %all-to-all-start.1 = ((bf16[128,2,2048]{2,1,0:T(2,128)(2,1)}), bf16[128,2,2048]{2,1,0:T(2,128)(2,1)S(1)}, u32[]{:S(2)}, u32[]{:S(2)}) async-start(bf16[128,2,2048]{2,1,0:T(2,128)(2,1)} %reshape.99), calls=%async_computation.1 | async-start | bytes 2097152 | tf_op jit(solution)/shard_map/all_to_all | solution.py:66
  50.9 0.0 reduce-scatter.2.cloned.1.call-start
  50.9 8.8 %copy.24 = bf16[2048,3,512]{0,2,1:T(8,128)(2,1)} copy(bf16[2048,3,512]{2,0,1:T(8,128)(2,1)} %param.10) | data formatting | bytes 12582912 | tf_op args[4]
  59.8 0.2 subtract_reduce_fusion
  60.0 0.1 sub.41
  60.1 20.1 %all-to-all-done.1 = bf16[128,2,2048]{2,1,0:T(2,128)(2,1)S(1)} async-done(((bf16[128,2,2048]{2,1,0:T(2,128)(2,1)}), bf16[128,2,2048]{2,1,0:T(2,128)(2,1)S(1)}, u32[]{:S(2)}, u32[]{:S(2)}) %all-to-all-start.1) | async-done | bytes 1048608 | tf_op jit(solution)/shard_map/all_to_all | solution.py:66
  80.2 1.2 reshape.131
  81.4 3.3 %scatter_custom_fusion = bf16[256,2048]{1,0:T(8,128)(2,1)S(1)} fusion(s32[256]{0:T(256)S(1)} %bitcast.44, bf16[256,2048]{1,0:T(8,128)(2,1)} %reshape.131, bf16[]{:T(256)} %constant.18.clone.1), kind=kCustom, calls=%fused_computation.27 | custom fusion | bytes 1049088 | tf_op jit(solution)/shard_map/scatter | solution.py:70
  84.7 5.5 %convolution_convert_fusion = bf16[256,1536]{1,0:T(8,128)(2,1)} fusion(bf16[256,2048]{1,0:T(8,128)(2,1)S(1)} %scatter_custom_fusion, bf16[2048,1536]{0,1:T(8,128)(2,1)} %bitcast.36), kind=kOutput, calls=%fused_computation.8 | convolution fusion | flops 1611005952 | bytes 8126464 | tf_op jit(solution)/shard_map/dot_general | solution.py:42
  90.2 2.3 %copy.25 = bf16[256,1536]{0,1:T(8,128)(2,1)} copy(bf16[256,1536]{1,0:T(8,128)(2,1)} %convolution_convert_fusion) | data formatting | bytes 1572864 | tf_op jit(solution)/shard_map/convert_element_type | solution.py:42
  92.5 2.0 %fusion.35 = (bf16[256,2,512]{0,2,1:T(8,128)(2,1)}, f32[256,2,512]{0,2,1:T(8,128)S(1)}) fusion(bf16[256,3,512]{0,2,1:T(8,128)(2,1)} %bitcast.38), kind=kLoop, calls=%fused_computation.69 | loop fusion | flops 262144 | bytes 2097152 | tf_op jit(solution)/shard_map/slice | solution.py:74
  94.5 1.3 copy.28
  95.8 1.5 bitcast_reduce_fusion
  97.3 1.0 collective-permute-start.4
  98.3 2.2 %collective-permute-done.4 = f32[16,2,512]{2,0,1:T(8,128)S(1)} collective-permute-done((f32[16,2,512]{2,0,1:T(8,128)S(1)}, f32[16,2,512]{2,0,1:T(8,128)S(1)}, u32[]{:S(2)}, u32[]{:S(2)}) %collective-permute-start.4) | collective-permute-done | bytes 65568 | tf_op jit(solution)/shard_map/ppermute | solution.py:31
  100.5 0.6 broadcast_select_fusion.5
  101.2 0.1 reshape.105
  101.3 0.2 reduce_sum.65
  101.5 0.6 collective-permute-start.5
  102.0 3.4 %collective-permute-start.2 = (s32[256]{0:T(256)S(1)}, s32[256]{0:T(256)S(1)}, u32[]{:S(2)}, u32[]{:S(2)}) collective-permute-start(s32[256]{0:T(256)S(1)} %broadcast_add_fusion), channel_id=1, source_target_pairs={{0,2},{2,4},{4,6},{6,8},{8,10},{10,12},{12,14},{14,16},{16,18},{18... | collective-permute-start | bytes 3080 | tf_op jit(solution)/shard_map/ppermute | solution.py:18
  105.4 1.3 collective-permute-start.3
  106.7 0.0 collective-permute-done.5
  106.7 0.6 broadcast_select_fusion.3
  107.3 0.1 reshape.106
  107.4 0.2 reduce_sum.66
  107.6 4.2 %collective-permute-start.6 = (f32[16,2,512]{2,0,1:T(8,128)S(1)}, f32[16,2,512]{2,0,1:T(8,128)S(1)}, u32[]{:S(2)}, u32[]{:S(2)}) collective-permute-start(f32[16,2,512]{2,0,1:T(8,128)S(1)} %broadcast_multiply_fusion.1), channel_id=1, source_target_pairs={{0,8},{8,0},{2,10},{10,2},{4,12},{12,4},{6,14},{14,6},{16,24},{24,... | collective-permute-start | bytes 196616 | tf_op jit(solution)/shard_map/ppermute | solution.py:31
  111.8 0.0 collective-permute-done.2
  111.8 0.0 collective-permute-done.3
  111.8 3.0 %collective-permute-done.6 = f32[16,2,512]{2,0,1:T(8,128)S(1)} collective-permute-done((f32[16,2,512]{2,0,1:T(8,128)S(1)}, f32[16,2,512]{2,0,1:T(8,128)S(1)}, u32[]{:S(2)}, u32[]{:S(2)}) %collective-permute-start.6) | collective-permute-done | bytes 65568 | tf_op jit(solution)/shard_map/ppermute | solution.py:31
  114.7 0.6 broadcast_select_fusion.1
  115.4 0.1 reshape.107
  115.5 0.2 reduce_sum.67
  115.7 2.1 %collective-permute-start.7 = (f32[16,2,512]{2,0,1:T(8,128)S(1)}, f32[16,2,512]{2,0,1:T(8,128)S(1)}, u32[]{:S(2)}, u32[]{:S(2)}) collective-permute-start(f32[16,2,512]{2,0,1:T(8,128)S(1)} %broadcast_multiply_fusion), channel_id=1, source_target_pairs={{0,16},{16,0},{2,18},{18,2},{4,20},{20,4},{6,22},{22,6},{8,24},{24... | collective-permute-start | bytes 196616 | tf_op jit(solution)/shard_map/ppermute | solution.py:31
  117.7 0.2 broadcast_compare_fusion
  117.9 1.0 slice.30
  118.9 2.8 %collective-permute-start = (bf16[256,2,512]{0,2,1:T(8,128)(2,1)S(1)}, bf16[256,2,512]{0,2,1:T(8,128)(2,1)}, u32[]{:S(2)}, u32[]{:S(2)}) collective-permute-start(bf16[256,2,512]{0,2,1:T(8,128)(2,1)S(1)} %copy-done.1), channel_id=1, source_target_pairs={{0,2},{2,4},{4,6},{6,8},{8,10},{10,12},{12,14},{14,16},{16,18},{18... | collective-permute-start | bytes 1572872 | tf_op jit(solution)/shard_map/ppermute | solution.py:18
  121.7 1.3 collective-permute-start.1
  123.0 0.0 collective-permute-done.7
  123.0 0.6 constant_dynamic-update-slice_fusion
  123.6 1.0 fusion.36
  124.7 0.3 fusion.37
  125.0 2.0 %collective-permute-done = bf16[256,2,512]{0,2,1:T(8,128)(2,1)} collective-permute-done((bf16[256,2,512]{0,2,1:T(8,128)(2,1)S(1)}, bf16[256,2,512]{0,2,1:T(8,128)(2,1)}, u32[]{:S(2)}, u32[]{:S(2)}) %collective-permute-start) | collective-permute-done | bytes 524320 | tf_op jit(solution)/shard_map/ppermute | solution.py:18
  127.0 4.7 %collective-permute-done.1 = bf16[256,2,512]{0,2,1:T(8,128)(2,1)} collective-permute-done((bf16[256,2,512]{0,2,1:T(8,128)(2,1)S(1)}, bf16[256,2,512]{0,2,1:T(8,128)(2,1)}, u32[]{:S(2)}, u32[]{:S(2)}) %collective-permute-start.1) | collective-permute-done | bytes 524320 | tf_op jit(solution)/shard_map/ppermute | solution.py:19
  131.7 1.3 pad_maximum_fusion
  133.0 0.1 fusion.34
  133.1 0.8 fusion
  134.0 0.1 fusion.27
  134.1 0.9 fusion.1
  135.0 0.6 fusion.28
  135.6 1.1 fusion.22
  136.8 2.1 %fusion.38 = f32[256,2048]{1,0:T(8,128)} fusion(bf16[256,512]{0,1:T(8,128)(2,1)S(1)} %bitcast.43, bf16[512,2048]{1,0:T(8,128)(2,1)S(1)} %copy-done), kind=kOutput, calls=%fused_computation.72 | convolution fusion | flops 536870912 | bytes 4456448 | tf_op jit(solution)/shard_map/dot_general | solution.py:125
  138.9 0.0 reduce-scatter.2.cloned.1.call-update
  138.9 25.5 %reduce-scatter.2.cloned.1.call-done = f32[256,1024]{1,0:T(8,128)} async-done(((f32[256,2048]{1,0:T(8,128)}), f32[256,1024]{1,0:T(8,128)}) %reduce-scatter.2.cloned.1.call-update) | async-done | bytes 1048592 | tf_op jit(solution)/shard_map/reduce_scatter | solution.py:126
  164.4 2.1 %convert_element_type.25 = bf16[256,1024]{1,0:T(8,128)(2,1)} convert(f32[256,1024]{1,0:T(8,128)} %reduce-scatter.2.cloned.1.call-done) | non-fusion elementwise | flops 262144 | bytes 1572864 | tf_op jit(solution)/shard_map/convert_element_type | solution.py:126
  (26 shorter events, 0.2 us)
Async XLA Ops:
  6.5 130.2 %copy-start = (bf16[512,2048]{1,0:T(8,128)(2,1)S(1)}, bf16[512,2048]{1,0:T(8,128)(2,1)}, u32[]{:S(2)}) copy-start(bf16[512,2048]{1,0:T(8,128)(2,1)} %param.11) | copy-start | bytes 6291460
  13.3 26.8 %all-to-all-start = ((s32[128,1,2]{2,1,0:T(1,128)}), s32[128,1,2]{2,1,0:T(1,128)S(1)}, u32[]{:S(2)}, u32[]{:S(2)}) async-start(s32[128,1,2]{2,1,0:T(1,128)} %bitcast), calls=%async_computation | async-start | bytes 131072 | tf_op jit(solution)/shard_map/all_to_all | solution.py:67
  40.1 40.1 %all-to-all-start.1 = ((bf16[128,2,2048]{2,1,0:T(2,128)(2,1)}), bf16[128,2,2048]{2,1,0:T(2,128)(2,1)S(1)}, u32[]{:S(2)}, u32[]{:S(2)}) async-start(bf16[128,2,2048]{2,1,0:T(2,128)(2,1)} %reshape.99), calls=%async_computation.1 | async-start | bytes 2097152 | tf_op jit(solution)/shard_map/all_to_all | solution.py:66
  50.9 113.5 %reduce-scatter.2.cloned.1.call-start = ((), (), s32[]{:S(2)}) async-start(), calls=%async_computation.3 | async-start | bytes 3145728 | tf_op jit(solution)/shard_map/reduce_scatter | solution.py:126
  92.5 9.5 %copy-start.2 = (s32[256]{0:T(256)S(1)}, s32[256]{0:T(256)}, u32[]{:S(2)}) copy-start(s32[256]{0:T(256)} %param.8) | copy-start | bytes 3076
  95.8 23.0 %copy-start.1 = (bf16[256,2,512]{0,2,1:T(8,128)(2,1)S(1)}, bf16[256,2,512]{0,2,1:T(8,128)(2,1)}, u32[]{:S(2)}) copy-start(bf16[256,2,512]{0,2,1:T(8,128)(2,1)} %get-tuple-element.9) | copy-start | bytes 1572868
  95.8 28.9 %copy-start.3 = (f32[64]{0:T(128)S(1)}, f32[64]{0:T(128)}, u32[]{:S(2)}) copy-start(f32[64]{0:T(128)} %constant.54.clone.1) | copy-start | bytes 772
  97.3 3.2 %collective-permute-start.4 = (f32[16,2,512]{2,0,1:T(8,128)S(1)}, f32[16,2,512]{2,0,1:T(8,128)S(1)}, u32[]{:S(2)}, u32[]{:S(2)}) collective-permute-start(f32[16,2,512]{2,0,1:T(8,128)S(1)} %broadcast_multiply_fusion.3), channel_id=1, source_target_pairs={{0,2},{2,0},{4,6},{6,4},{8,10},{10,8},{12,14},{14,12},{16,18},{18,... | collective-permute-start | bytes 196616 | tf_op jit(solution)/shard_map/ppermute | solution.py:31
  101.5 5.2 %collective-permute-start.5 = (f32[16,2,512]{2,0,1:T(8,128)S(1)}, f32[16,2,512]{2,0,1:T(8,128)S(1)}, u32[]{:S(2)}, u32[]{:S(2)}) collective-permute-start(f32[16,2,512]{2,0,1:T(8,128)S(1)} %broadcast_multiply_fusion.2), channel_id=1, source_target_pairs={{0,4},{4,0},{2,6},{6,2},{8,12},{12,8},{10,14},{14,10},{16,20},{20,... | collective-permute-start | bytes 196616 | tf_op jit(solution)/shard_map/ppermute | solution.py:31
  102.0 9.8 %collective-permute-start.2 = (s32[256]{0:T(256)S(1)}, s32[256]{0:T(256)S(1)}, u32[]{:S(2)}, u32[]{:S(2)}) collective-permute-start(s32[256]{0:T(256)S(1)} %broadcast_add_fusion), channel_id=1, source_target_pairs={{0,2},{2,4},{4,6},{6,8},{8,10},{10,12},{12,14},{14,16},{16,18},{18... | collective-permute-start | bytes 3080 | tf_op jit(solution)/shard_map/ppermute | solution.py:18
  105.4 6.4 %collective-permute-start.3 = (s32[256]{0:T(256)S(1)}, s32[256]{0:T(256)S(1)}, u32[]{:S(2)}, u32[]{:S(2)}) collective-permute-start(s32[256]{0:T(256)S(1)} %broadcast_add_fusion), channel_id=1, source_target_pairs={{2,0},{4,2},{6,4},{8,6},{10,8},{12,10},{14,12},{16,14},{18,16},{20... | collective-permute-start | bytes 3080 | tf_op jit(solution)/shard_map/ppermute | solution.py:19
  107.6 7.1 %collective-permute-start.6 = (f32[16,2,512]{2,0,1:T(8,128)S(1)}, f32[16,2,512]{2,0,1:T(8,128)S(1)}, u32[]{:S(2)}, u32[]{:S(2)}) collective-permute-start(f32[16,2,512]{2,0,1:T(8,128)S(1)} %broadcast_multiply_fusion.1), channel_id=1, source_target_pairs={{0,8},{8,0},{2,10},{10,2},{4,12},{12,4},{6,14},{14,6},{16,24},{24,... | collective-permute-start | bytes 196616 | tf_op jit(solution)/shard_map/ppermute | solution.py:31
  115.7 7.3 %collective-permute-start.7 = (f32[16,2,512]{2,0,1:T(8,128)S(1)}, f32[16,2,512]{2,0,1:T(8,128)S(1)}, u32[]{:S(2)}, u32[]{:S(2)}) collective-permute-start(f32[16,2,512]{2,0,1:T(8,128)S(1)} %broadcast_multiply_fusion), channel_id=1, source_target_pairs={{0,16},{16,0},{2,18},{18,2},{4,20},{20,4},{6,22},{22,6},{8,24},{24... | collective-permute-start | bytes 196616 | tf_op jit(solution)/shard_map/ppermute | solution.py:31
  118.9 8.1 %collective-permute-start = (bf16[256,2,512]{0,2,1:T(8,128)(2,1)S(1)}, bf16[256,2,512]{0,2,1:T(8,128)(2,1)}, u32[]{:S(2)}, u32[]{:S(2)}) collective-permute-start(bf16[256,2,512]{0,2,1:T(8,128)(2,1)S(1)} %copy-done.1), channel_id=1, source_target_pairs={{0,2},{2,4},{4,6},{6,8},{8,10},{10,12},{12,14},{14,16},{16,18},{18... | collective-permute-start | bytes 1572872 | tf_op jit(solution)/shard_map/ppermute | solution.py:18
  121.7 10.0 %collective-permute-start.1 = (bf16[256,2,512]{0,2,1:T(8,128)(2,1)S(1)}, bf16[256,2,512]{0,2,1:T(8,128)(2,1)}, u32[]{:S(2)}, u32[]{:S(2)}) collective-permute-start(bf16[256,2,512]{0,2,1:T(8,128)(2,1)S(1)} %copy-done.1), channel_id=1, source_target_pairs={{2,0},{4,2},{6,4},{8,6},{10,8},{12,10},{14,12},{16,14},{18,16},{20... | collective-permute-start | bytes 1572872 | tf_op jit(solution)/shard_map/ppermute | solution.py:19
Sparse Core Ops, SparseCore 0:
  139.0 25.3 reduce-scatter.1
where the time goes:
time: 174 us; the launch traced here: 173 us
  waiting for transfers between devices  60 us (34%)
  starting transfers between devices  43.6 us (25%)
  local copies, waits for them, and re-layouts  27.8 us (16%)
  other arithmetic  17.7 us (10%)
  between operations  13.7 us (8%)
  matrix products  10.5 us (6%)
    reduce_scatter x1, waiting for transfers between devices, shards(): lax.psum_scatter(partial_out, 'head', scatter_dimension=1, tiled=True)  25.5 us
    all_to_all x1, waiting for transfers between devices, shards(): lax.all_to_all(sending, 'seq', split_axis=0, concat_axis=0, tiled=True)  20.1 us
    all_to_all x1, starting transfers between devices, shards(): lax.all_to_all(sent_pos, 'seq', split_axis=0, concat_axis=0, tiled=True)  16.3 us
    all_to_all x1, starting transfers between devices, shards(): lax.all_to_all(sending, 'seq', split_axis=0, concat_axis=0, tiled=True)  10.7 us
    unnamed x9, local copies, waits for them, and re-layouts  8.86 us
    ppermute x4, starting transfers between devices, from_partner(): return lax.ppermute(block, axis, route)  7.78 us
    ppermute x2, starting transfers between devices, extended(): before = lax.ppermute(last, axis, up)  6.18 us
    dot_general x1, matrix products, project(): jnp.dot(normed, w_qkv.reshape(width, -1), preferred_element_type=jnp.floa...  5.5 us
  transfers between devices with their start and end apart: 11, of which 7 were waited for; matrix products, arithmetic and copies ran while one was open for 12% of the time, Pallas kernels for 0%

commit v1 on v0

v1 whole, which is shorter than its diff:
```python
import functools
import math

import jax
import jax.numpy as jnp
from jax import lax
from jax.experimental import pallas as pl
from jax.experimental.pallas import tpu as pltpu
from jax.sharding import PartitionSpec as P

MESH = pl.DeviceIdType.MESH
F32 = jnp.float32
BF16 = jnp.bfloat16
NX, NY, NZ = 4, 4, 8
NXY = NX * NY
SHARDS = NXY * NZ
ROWS = 256
WIDTH = 2048
DH = 128
GROUP = 512
HEADS = 4
CHUNKS = WIDTH // 128
SCORE = DH ** (-0.5) * math.log2(math.e)
Z_ORDER = (4, 3, 5, 2, 6, 1, 7, 0)


def iota(shape, dim):
    return lax.broadcasted_iota(jnp.int32, shape, dim)


def mm(a, b):
    return jnp.dot(a, b, preferred_element_type=F32)


def mm_nt(a, b):
    return lax.dot_general(a, b, (((1,), (1,)), ((), ())), preferred_element_type=F32)


def layer(
    tok_hbm, dest_ref, seg_ref, gain_ref, wqkv_hbm, wout_hbm, out_ref,
    tok, wqkv, wo_own, wo_sib, stage, send, recv, recv_sib, xs,
    posa_src, posa, posb_src, posb, place, pool,
    k_own, v_own, q_raw, q_own, ids_src, ids_halo, k_halo, v_halo,
    crs_src, crs, bias, top, tot, acc, prob, at_own, at_sib,
    load_sem, row_send, row_recv, sib_send, sib_recv,
    pos_sem, ids_sem, k_send, k_recv, v_send, v_recv, crs_sem, wo_sem, at_sem,
):
    me = lax.axis_index("seq")
    core = lax.axis_index("head")
    other = 1 - core
    xy, z = me // NZ, me % NZ
    y, x = xy // NX, xy % NX
    left, right = (me + SHARDS - 1) % SHARDS, (me + 1) % SHARDS

    def remote(src, dst, send_sem, recv_sem, seq, head):
        return pltpu.make_async_remote_copy(
            src_ref=src, dst_ref=dst, send_sem=send_sem, recv_sem=recv_sem,
            device_id=(seq, head), device_id_type=MESH,
        )

    def drain(ref, sem):
        pltpu.make_async_copy(ref, ref, sem).wait()

    load_tok = pltpu.make_async_copy(tok_hbm, tok, load_sem.at[0])
    load_tok.start()
    load_w = [
        pltpu.make_async_copy(wqkv_hbm.at[part], wqkv.at[part], load_sem.at[1 + part])
        for part in range(3)
    ]
    for part in (1, 2, 0):
        load_w[part].start()
    load_wo = pltpu.make_async_copy(
        wout_hbm.at[:, pl.ds(pl.multiple_of(core * 1024, 1024), 1024)], wo_own, load_sem.at[4]
    )
    load_wo.start()

    barrier = pltpu.get_barrier_semaphore()

    def greet(i, carry):
        pl.semaphore_signal(
            barrier, inc=1, device_id=((me + 1 + i) % SHARDS, core), device_id_type=MESH
        )
        return carry

    lax.fori_loop(0, SHARDS - 1, greet, 0)
    pl.semaphore_signal(barrier, inc=1, device_id=(me, other), device_id_type=MESH)

    dest = dest_ref[...]
    shard = jnp.right_shift(dest, 8).astype(F32)
    slot = jnp.bitwise_and(dest, 255).astype(F32)
    by_lane = jnp.broadcast_to(shard, (ROWS, ROWS))
    by_row = by_lane.T
    earlier = (by_lane == by_row) & (iota((ROWS, ROWS), 0) < iota((ROWS, ROWS), 1))
    rank = jnp.sum(jnp.where(earlier, 1.0, 0.0), axis=0, keepdims=True)
    hit = iota((SHARDS, ROWS), 0).astype(F32) == shard
    mine = hit & (rank == core.astype(F32))
    pick = jnp.where(mine, 1.0, 0.0).astype(BF16)
    pair = iota((8, ROWS), 0).astype(F32) == rank
    slots = jnp.where(pair, slot, 0.0).astype(BF16)
    posa_src[...] = mm_nt(slots, jnp.where(hit, 1.0, 0.0).astype(BF16))
    load_tok.wait()
    gain = gain_ref[...]
    rows = mm(pick, tok[...])
    scale = lax.rsqrt(jnp.sum(rows * rows, axis=-1, keepdims=True) * (1.0 / WIDTH) + 1e-05)
    for j in range(CHUNKS):
        cols = slice(j * 128, (j + 1) * 128)
        stage[pl.ds(j, SHARDS, stride=CHUNKS), :] = rows[:, cols] * scale * gain[:, cols]
    send[...] = stage[...].reshape(SHARDS, CHUNKS, 128).astype(BF16)

    pl.semaphore_wait(barrier, SHARDS)

    posa[pl.ds(pl.multiple_of(z * 8, 8), 8), :] = posa_src[...]
    for o in range(1, NZ):
        remote(
            posa_src, posa.at[pl.ds(pl.multiple_of(z * 8, 8), 8)], pos_sem.at[0], pos_sem.at[1],
            xy * NZ + (z + o) % NZ, core,
        ).start()

    def offsets(i):
        return (i // NX + 1) % NX, (i % NX + 1) % NX

    def send_rows(i, skip_self):
        ox, oy = offsets(i)
        base = (((y + oy) % NY) * NX + (x + ox) % NX) * NZ
        for oz in Z_ORDER:
            if skip_self and oz == 0:
                continue
            peer = base + (z + oz) % NZ
            remote(
                send.at[peer], recv.at[me], row_send, row_recv.at[i], peer, core
            ).start()

    def send_loop(i, carry):
        send_rows(i, False)
        return carry

    lax.fori_loop(0, NXY - 1, send_loop, 0)
    send_rows(NXY - 1, True)
    pltpu.make_async_copy(send.at[me], recv.at[me], row_recv.at[NXY - 1]).start()

    remote(
        wout_hbm.at[:, pl.ds(pl.multiple_of(other * 1024, 1024), 1024)], wo_sib,
        wo_sem.at[0], wo_sem.at[1], me, other,
    ).start()

    drain(posa.at[pl.ds(0, 56)], pos_sem.at[1])
    for k in range(2):
        posb_src[k * 8:(k + 1) * 8, :] = posa[pl.ds(k, 8, stride=8), :]
    posb[pl.ds(pl.multiple_of(xy * 16, 16), 16), :] = posb_src[...]

    def send_pos(o, carry):
        remote(
            posb_src, posb.at[pl.ds(pl.multiple_of(xy * 16, 16), 16)], pos_sem.at[2],
            pos_sem.at[3], ((xy + o) % NXY) * NZ + z, core,
        ).start()
        return carry

    lax.fori_loop(1, NXY, send_pos, 0)
    drain(posb.at[pl.ds(0, 240)], pos_sem.at[3])
    table = posb[...].reshape(NXY, 16, 128)
    my_lane = jnp.where(iota((8, 128), 1) == me, 1.0, 0.0).astype(BF16)
    found = [
        mm_nt(my_lane, table[:, k * 8:(k + 1) * 8, :].reshape(SHARDS, 128).astype(BF16))
        for k in range(2)
    ]
    first = core == 0
    pos = jnp.concatenate(
        [jnp.where(first, found[0], found[1]), jnp.where(first, found[1], found[0])], axis=1
    )
    pos_row = pos[0:1, :]
    where_to = jnp.where(iota((ROWS, ROWS), 0).astype(F32) == pos_row, 1.0, 0.0).astype(BF16)
    place[...] = where_to
    seg = seg_ref[...].astype(F32)
    ids_src[...] = mm(jnp.broadcast_to(seg, (8, ROWS)).astype(BF16), where_to)
    for side, peer in ((1, left), (0, right)):
        remote(ids_src, ids_halo.at[side], ids_sem.at[0], ids_sem.at[1], peer, core).start()

    place_int = pos_row.astype(jnp.int32)
    line = iota((128, ROWS), 0)
    spread = jnp.broadcast_to(place_int, (128, ROWS))
    weights = jnp.zeros((128, ROWS), F32)
    start = 0
    for level in range(4):
        count = 16 >> level
        inside = (line >= start) & (line < start + HEADS * count)
        same = jnp.right_shift(spread, 4 + level) == (line - start) % count
        weights = jnp.where(inside & same, 1.0 / (16 << level), weights)
        start += HEADS * count
    pool[...] = weights.astype(BF16)

    own_col = jnp.broadcast_to(seg, (ROWS, ROWS)).T
    bias[:, 0:ROWS] = jnp.where(own_col == ids_src[0:1, :], 0.0, -jnp.inf)

    def share(i, carry):
        ox, oy = offsets(i)
        base = (((y + NY - oy) % NY) * NX + (x + NX - ox) % NX) * NZ
        block = pl.ds(base, NZ)
        drain(recv.at[block], row_recv.at[i])
        remote(recv.at[block], recv_sib.at[block], sib_send, sib_recv, me, other).start()
        return carry

    lax.fori_loop(0, NXY, share, 0)
    stage[...] = recv[...].astype(F32).reshape(SHARDS * CHUNKS, 128)
    for j in range(CHUNKS):
        xs[0:128, j * 128:(j + 1) * 128] = stage[pl.ds(j, SHARDS, stride=CHUNKS), :].astype(BF16)
    drain(recv_sib, sib_recv)
    stage[...] = recv_sib[...].astype(F32).reshape(SHARDS * CHUNKS, 128)
    for j in range(CHUNKS):
        xs[128:256, j * 128:(j + 1) * 128] = stage[pl.ds(j, SHARDS, stride=CHUNKS), :].astype(BF16)

    for part, own, halo, send_sem, recv_sem in (
        (1, k_own, k_halo, k_send, k_recv), (2, v_own, v_halo, v_send, v_recv)
    ):
        load_w[part].wait()
        for half in range(2):
            cols = slice(half * 256, (half + 1) * 256)
            own[half] = mm(xs[...], wqkv[part, :, cols]).astype(BF16)
            for side, peer in ((1, left), (0, right)):
                remote(
                    own.at[half], halo.at[side, half], send_sem, recv_sem.at[side, half], peer, core
                ).start()

    line = iota((128, 128), 0)
    head_of = jnp.where(
        line < 64, line // 16,
        jnp.where(line < 96, (line - 64) // 8, jnp.where(line < 112, (line - 96) // 4, (line - 112) // 2)),
    )
    for which, own in ((0, k_own), (1, v_own)):
        picked = jnp.zeros((128, 128), F32)
        for half in range(2):
            means = mm(pool[...], own[half])
            for sub in range(2):
                picked = jnp.where(
                    head_of == half * 2 + sub, means[:, sub * 128:(sub + 1) * 128], picked
                )
        crs_src[:, which * 128:(which + 1) * 128] = picked.astype(BF16)
    start = 0
    for level in range(4):
        size = 1 << level
        lines = 64 >> level
        group = me // size
        partner = group + 1 - 2 * (group % 2)
        for i in range(size):
            remote(
                crs_src.at[pl.ds(start, lines)],
                crs.at[pl.ds(pl.multiple_of(64 * level + (me % size) * lines, 8), lines)],
                crs_sem.at[0], crs_sem.at[1], partner * size + i, core,
            ).start()
        start += lines

    load_w[0].wait()
    for half in range(2):
        cols = slice(half * 256, (half + 1) * 256)
        q_raw[half] = mm(xs[...], wqkv[0, :, cols]).astype(BF16)
    for half in range(2):
        q_own[half] = mm(place[...], q_raw[half]).astype(BF16)

    def head(ref, h):
        return ref[h // 2, :, (h % 2) * 128:(h % 2 + 1) * 128]

    def fine(h, keys, mask):
        return mm_nt(head(q_own, h), keys) * SCORE + mask

    for h in range(HEADS):
        score = fine(h, head(k_own, h), bias[:, 0:ROWS])
        best = jnp.max(score, axis=-1, keepdims=True)
        weight = jnp.exp2(score - best)
        tot[h] = jnp.broadcast_to(jnp.sum(weight, axis=-1, keepdims=True), (ROWS, 128))
        top[h] = jnp.broadcast_to(best, (ROWS, 128))
        acc[h] = mm(weight.astype(BF16), head(v_own, h))

    drain(ids_halo, ids_sem.at[1])
    own_col = jnp.broadcast_to(seg, (ROWS, ROWS)).T
    edge = ((me > 0), (me < SHARDS - 1))
    for side in range(2):
        same = own_col == ids_halo[side][0:1, :]
        bias[:, (side + 1) * ROWS:(side + 2) * ROWS] = jnp.where(same & edge[side], 0.0, -jnp.inf)

    drain(crs, crs_sem.at[1])
    lane = iota((8, 256), 1)
    level_of = lane // 64
    holder = jnp.where(
        level_of == 0, (lane % 64) // 16,
        jnp.where(level_of == 1, (lane % 32) // 8, jnp.where(level_of == 2, (lane % 16) // 4, (lane % 8) // 2)),
    )
    lift = (level_of + 4).astype(F32)
    for h in range(HEADS):
        far_mask = jnp.where(holder == h, lift, -jnp.inf)[0:1, :]
        score = fine(h, crs[:, 0:128], far_mask)
        old = top[h][:, 0:1]
        best = jnp.maximum(old, jnp.max(score, axis=-1, keepdims=True))
        weight = jnp.exp2(score - best)
        fade = jnp.exp2(old - best)
        tot[h] = tot[h] * fade + jnp.sum(weight, axis=-1, keepdims=True)
        top[h] = jnp.broadcast_to(best, (ROWS, 128))
        acc[h] = acc[h] * fade + mm(weight.astype(BF16), crs[:, 128:256])

    for half in range(2):
        for side in range(2):
            drain(k_halo.at[side, half], k_recv.at[side, half])
        for h in (half * 2, half * 2 + 1):
            cols = slice((h % 2) * 128, (h % 2 + 1) * 128)
            scores = [
                fine(h, k_halo[side, half, :, cols], bias[:, (side + 1) * ROWS:(side + 2) * ROWS])
                for side in range(2)
            ]
            old = top[h][:, 0:1]
            best = old
            for score in scores:
                best = jnp.maximum(best, jnp.max(score, axis=-1, keepdims=True))
            fade = jnp.exp2(old - best)
            total = tot[h] * fade
            for side in range(2):
                weight = jnp.exp2(scores[side] - best)
                total = total + jnp.sum(weight, axis=-1, keepdims=True)
                prob[h, side] = weight.astype(BF16)
            tot[h] = total
            acc[h] = acc[h] * fade

    load_wo.wait()
    for half in range(2):
        for side in range(2):
            drain(v_halo.at[side, half], v_recv.at[side, half])
        for h in (half * 2, half * 2 + 1):
            cols = slice((h % 2) * 128, (h % 2 + 1) * 128)
            total = acc[h]
            for side in range(2):
                total = total + mm(prob[h, side], v_halo[side, half, :, cols])
            at_own[half, :, cols] = (total / tot[h]).astype(BF16)
        remote(
            at_own.at[half], at_sib.at[half], at_sem.at[0], at_sem.at[1 + half], me, other
        ).start()

    drain(wo_sib, wo_sem.at[1])
    for half in range(2):
        drain(at_sib.at[half], at_sem.at[1 + half])
    for part in range(4):
        cols = slice(part * 256, (part + 1) * 256)
        total = jnp.zeros((ROWS, 256), F32)
        for half in range(2):
            lines = slice(half * 256, (half + 1) * 256)
            total = total + mm(at_own[half], wo_own[lines, cols])
            total = total + mm(at_sib[half], wo_sib[lines, cols])
        out_ref[:, cols] = total.astype(BF16)

    drain(send.at[pl.ds(0, SHARDS - 1)], row_send)
    drain(posa.at[pl.ds(0, 56)], pos_sem.at[0])
    drain(posb.at[pl.ds(0, 240)], pos_sem.at[2])
    drain(ids_halo, ids_sem.at[0])
    drain(recv, sib_send)
    drain(k_halo, k_send)
    drain(v_halo, v_send)
    drain(crs, crs_sem.at[0])
    drain(wo_sib, wo_sem.at[0])
    drain(at_own, at_sem.at[0])


def shards(tokens, dest, segment_ids, gain, w_qkv, w_out):
    vmem = pl.BlockSpec(memory_space=pltpu.VMEM)
    hbm = pl.BlockSpec(memory_space=pl.ANY)
    dma = pltpu.SemaphoreType.DMA
    V = pltpu.VMEM
    return pl.pallas_call(
        layer,
        out_shape=jax.ShapeDtypeStruct((ROWS, 1024), BF16),
        in_specs=[hbm, vmem, vmem, vmem, hbm, hbm],
        out_specs=vmem,
        scratch_shapes=[
            V((ROWS, WIDTH), BF16), V((3, WIDTH, GROUP), BF16), V((GROUP, 1024), BF16),
            V((GROUP, 1024), BF16), V((SHARDS * CHUNKS, 128), F32), V((SHARDS, CHUNKS, 128), BF16),
            V((SHARDS, CHUNKS, 128), BF16), V((SHARDS, CHUNKS, 128), BF16), V((ROWS, WIDTH), BF16),
            V((8, 128), F32), V((64, 128), F32), V((16, 128), F32), V((256, 128), F32),
            V((ROWS, ROWS), BF16), V((128, ROWS), BF16),
            V((2, ROWS, 256), BF16), V((2, ROWS, 256), BF16), V((2, ROWS, 256), BF16),
            V((2, ROWS, 256), BF16), V((8, ROWS), F32), V((2, 8, ROWS), F32),
            V((2, 2, ROWS, 256), BF16), V((2, 2, ROWS, 256), BF16),
            V((128, 256), BF16), V((256, 256), BF16), V((ROWS, 3 * ROWS), F32),
            V((HEADS, ROWS, 128), F32), V((HEADS, ROWS, 128), F32), V((HEADS, ROWS, 128), F32),
            V((HEADS, 2, ROWS, ROWS), BF16), V((2, ROWS, 256), BF16), V((2, ROWS, 256), BF16),
            dma((5,)), dma, dma((NXY,)), dma, dma,
            dma((4,)), dma((2,)), dma, dma((2, 2)), dma, dma((2, 2)), dma((2,)), dma((2,)), dma((3,)),
        ],
        compiler_params=pltpu.CompilerParams(collective_id=0, has_side_effects=True),
    )(
        tokens, dest.reshape(1, ROWS), segment_ids.reshape(1, ROWS), gain.reshape(1, WIDTH),
        jnp.transpose(w_qkv, (1, 0, 2)), w_out,
    )


def solution(mesh):
    in_specs = (P("seq", None), P("seq"), P("seq"), P(), P(None, None, "head"), P("head", None))
    return jax.shard_map(
        shards, mesh=mesh, in_specs=in_specs, out_specs=P("seq", "head"), check_vma=False
    )
```

time: 174 us -> 60.5 us (0.35)
  waiting for transfers between devices: 60 us -> 0 us
  Pallas kernels: 0 us -> 58.5 us
  starting transfers between devices: 43.6 us -> 0 us
  local copies, waits for them, and re-layouts: 27.8 us -> 1.87 us
  other arithmetic: 17.7 us -> 0 us
  between operations: 13.7 us -> 0.01 us
  matrix products: 10.5 us -> 0 us
    pallas_call x0 -> x1, Pallas kernels: none -> 58.5 us  [shards(): pl.pallas_call(layer, out_shape=jax.ShapeDtypeStruct((ROWS, 1024), BF16),...]
    all_to_all x2 -> x0, starting transfers between devices: 27.1 us -> none  [the longest x1 16.3 us: shards(): lax.all_to_all(sent_pos, 'seq', split_axis=0, concat_axis=0, tiled=True)]
    reduce_scatter x1 -> x0, waiting for transfers between devices: 25.5 us -> none  [shards(): lax.psum_scatter(partial_out, 'head', scatter_dimension=1, tiled=True)]
    all_to_all x2 -> x0, waiting for transfers between devices: 22.6 us -> none  [the longest x1 20.1 us: shards(): lax.all_to_all(sending, 'seq', split_axis=0, concat_axis=0, tiled=True)]
    ppermute x8 -> x0, starting transfers between devices: 16.5 us -> none  [the longest x4 7.78 us: from_partner(): return lax.ppermute(block, axis, route)]
    ppermute x8 -> x0, waiting for transfers between devices: 11.9 us -> none  [the longest x4 5.17 us: from_partner(): return lax.ppermute(block, axis, route)]
    dot_general x6 -> x0, matrix products: 10.5 us -> none  [the longest x1 5.5 us: project(): jnp.dot(normed, w_qkv.reshape(width, -1), preferred_element_type=jnp.floa...]
    unnamed x9 -> x1, local copies, waits for them, and re-layouts: 8.86 us -> 1.87 us
  transfers between devices with their start and end apart: 11 -> 0, of which waited for: 7 -> 0; matrix products, arithmetic and copies ran while one was open for 12% -> 0% of each run, Pallas kernels for 0% -> 0%
where the time goes in v1:
time: 60.5 us; the launch traced here: 60.3 us
  Pallas kernels  58.5 us (97%)
  local copies, waits for them, and re-layouts  1.87 us (3%)
    pallas_call x1, Pallas kernels, shards(): pl.pallas_call(layer, out_shape=jax.ShapeDtypeStruct((ROWS, 1024), BF16),...  58.5 us
    unnamed x1, local copies, waits for them, and re-layouts  1.87 us

profile of v1, /device:TPU:1, one launch (start us, length us, event | category | flops | bytes accessed | tf_op | source)
XLA Modules:
  0.0 60.3 jit_solution(4800251168528501977)
XLA Ops:
  0.0 58.5 %shard_map.64 = bf16[256,1024]{1,0:T(8,128)(2,1)} custom-call(bf16[256,2048]{1,0:T(8,128)(2,1)} %tok_hbm.1, s32[1,256]{1,0:T(1,128)} %bitcast.6, s32[1,256]{1,0:T(1,128)} %bitcast.7, f32[1,2048]{1,0:T(1,128)} %bitcast.5, bf16[3,2048,512]{2,1,0:T(8,128)(2,1)} %bitcast.4, bf16[512,2048]{1,0:T(8,128)(2,1)} %wout_hbm.1), custom_call_target="tpu_custom_call" | custom-call | tf_op jit(solution)/shard_map/pallas_call | solution.py:363
  58.5 1.9 %copy.8 = bf16[256,1024]{1,0:T(8,128)(2,1)} copy(bf16[256,1024]{1,0:T(8,128)(2,1)} %shard_map.64) | data formatting | bytes 1048576
